TPU v7x, 256 devices: a whole 4x4x8 slice. The times are simulated.
256 devices in a mesh: member: 16 (over y, x_hi, core), domain: 16 (over x_lo, z).
Axes of the slice: x: 4 (x_hi: 2, x_lo: 2; x = x_hi * 2 + x_lo), y: 4, z: 8, core: 2. Of those that a mesh axis runs over, the one named last changes fastest.
Arguments:
- state: float32 [16, 4, 512, 512], P('member', None, 'domain'), may hold values from -5 to 5
- perturbation: float32 [16, 4, 512, 512], P('member', None, 'domain'), may hold values from -3 to 3
- parents: int32 [16], replicated, may hold values from 0 to 15
Outputs:
- final_state: float32 [16, 4, 512, 512], P('member', None, 'domain')
- score: float32 [16], P('member')
Inputs may be any that keep to these rules, and one draw needn't show every extreme that they name: `parents`: A member may be the parent of several slots or of none.
All inputs are finite; a program needn't handle non-finite values.
Results may differ from a plain program's by a relative error of at most 0.00002.
Values sent between devices are 32-bit elements; how exact they have to be, the bound alone decides.
A program may use at most 64 MiB of HBM per device.

v0:
```python
import jax
import jax.numpy as jnp
from jax import lax
from jax.sharding import PartitionSpec as P

STEPS = 3
time_step = 0.1
viscous = 0.05
coriolis = 1.0


def with_halo(cells, sides, width):
    for axis, dim in sides:
        count = lax.axis_size(axis)
        ends = count - 1
        head = lax.slice_in_dim(cells, 0, width, axis=dim)
        tail = lax.slice_in_dim(cells, cells.shape[dim] - width, cells.shape[dim], axis=dim)
        cells = jnp.concatenate(
            [
                lax.ppermute(tail, axis, [(i, (i + 1) % count) for i in range(ends)]),
                cells,
                lax.ppermute(head, axis, [((i + 1) % count, i) for i in range(ends)]),
            ],
            axis=dim,
        )
    return cells


def gradients(padded):
    middle = padded[:, 1:-1]
    east = jnp.roll(middle, -1, axis=-1)
    west = jnp.roll(middle, 1, axis=-1)
    return (middle, east, west, padded[:, 2:], padded[:, :-2])


def tendency(padded, start_row, total_rows):
    middle, east, west, north, south = gradients(padded)
    grad_x = (east - west) * 0.5
    grad_y = (north - south) * 0.5
    laplace = east + west + north + south - 4.0 * middle
    depth = 1.0 + padded[0]
    fluxes = jnp.stack([depth * padded[1], depth * padded[2]])
    flux_mid, flux_east, flux_west, flux_north, flux_south = gradients(fluxes)
    count = padded.shape[1] - 2
    global_rows = (start_row + 1 + jnp.arange(count, dtype=jnp.int32)).astype(jnp.float32)
    latitude = coriolis * (2.0 * (global_rows + 0.5) / total_rows - 1.0)
    latitude = latitude[:, None]
    height, speed_u, speed_v, tracer = (middle[0], middle[1], middle[2], middle[3])
    advect = speed_u * grad_x + speed_v * grad_y
    d_eta = (
        -((flux_east[0] - flux_west[0]) * 0.5 + (flux_north[1] - flux_south[1]) * 0.5)
        + viscous * laplace[0]
    )
    d_u = -advect[1] + latitude * speed_v - grad_x[0] + viscous * laplace[1]
    d_v = -advect[2] - latitude * speed_u - grad_y[0] + viscous * laplace[2]
    d_q = -advect[3] + viscous * laplace[3]
    return jnp.stack([d_eta, d_u, d_v, d_q])


def section_operator(field, first_row, total_rows):
    padded = with_halo(field, (("domain", 1),), 1)
    return tendency(padded, first_row - 1, total_rows)


def step_shallow(field, first_row, total_rows):
    start = section_operator(field, first_row, total_rows)
    first = field + time_step * start
    second = 0.75 * field + 0.25 * (
        first + time_step * section_operator(first, first_row, total_rows)
    )
    return 1.0 / 3.0 * field + 2.0 / 3.0 * (
        second + time_step * section_operator(second, first_row, total_rows)
    )


def run_steps(field, first_row, total_rows):
    for count in range(STEPS):
        field = step_shallow(field, first_row, total_rows)
    return field


def on_device(state, perturbation, parents):
    rows = state.shape[2]
    width = state.shape[3]
    total_rows = rows * lax.axis_size("domain")
    first_row = lax.axis_index("domain") * rows
    before = run_steps(state[0], first_row, total_rows)
    global_rows = (first_row + jnp.arange(rows, dtype=jnp.int32)).astype(jnp.float32)
    weight = 1.0 + 2.0 * global_rows / (total_rows - 1)
    local_score = jnp.sum(weight[:, None] * before[3] * before[3])
    score = lax.psum(local_score, "domain") / (total_rows * width)
    parent = lax.dynamic_index_in_dim(parents, lax.axis_index("member"), 0, keepdims=False)
    piece = lax.all_gather(before[None], "member", axis=0, tiled=True)
    count = piece.shape[0]
    inside = (parent >= 0) & (parent < count)
    chosen = lax.dynamic_index_in_dim(piece, jnp.clip(parent, 0, count - 1), 0, keepdims=False)
    cloned = jnp.where(inside, chosen, jnp.zeros_like(before))
    after = run_steps(cloned + perturbation[0], first_row, total_rows)
    return (after[None], jnp.reshape(score, (1,)))


def solution(mesh):
    placed = (P("member", None, "domain", None), P("member", None, "domain", None), P())
    return jax.shard_map(
        on_device,
        mesh=mesh,
        in_specs=placed,
        out_specs=(P("member", None, "domain", None), P("member")),
        check_vma=False,
    )
```

profile of v0, /device:TPU:2, one launch (start us, length us, event | category | flops | bytes accessed | tf_op | source)
XLA Modules:
  0.0 271.7 jit_solution(4103556976015861069)
XLA Ops:
  7.2 0.9 fusion.504
  8.1 3.8 %collective-permute-start = (f32[4,1,512]{2,1,0:T(1,128)S(1)}, f32[4,1,512]{2,1,0:T(1,128)S(1)}, u32[]{:S(2)}, u32[]{:S(2)}) collective-permute-start(f32[4,1,512]{2,1,0:T(1,128)S(1)} %get-tuple-element.324), channel_id=1, source_target_pairs={{0,1},{1,2},{2,3},{3,4},{4,5},{5,6},{6,7},{7,8},{8,9},{9,10},{10,1... | collective-permute-start | bytes 24584 | tf_op jit(solution)/shard_map/ppermute | solution.py:20
  12.0 5.8 %collective-permute-start.1 = (f32[4,1,512]{2,1,0:T(1,128)S(1)}, f32[4,1,512]{2,1,0:T(1,128)S(1)}, u32[]{:S(2)}, u32[]{:S(2)}) collective-permute-start(f32[4,1,512]{2,1,0:T(1,128)S(1)} %get-tuple-element.325), channel_id=1, source_target_pairs={{1,0},{2,1},{3,2},{4,3},{5,4},{6,5},{7,6},{8,7},{9,8},{10,9},{11,1... | collective-permute-start | bytes 24584 | tf_op jit(solution)/shard_map/ppermute | solution.py:22
  17.8 1.2 fusion.502
  19.0 1.0 fusion.503
  19.9 0.9 multiply_bitcast_fusion.35
  20.9 0.9 maximum_multiply_fusion.51
  22.0 1.4 multiply_add_fusion.17
  23.8 1.9 collective-permute-start.2
  25.7 6.0 %collective-permute-start.3 = (f32[4,1,512]{2,1,0:T(1,128)S(1)}, f32[4,1,512]{2,1,0:T(1,128)S(1)}, u32[]{:S(2)}, u32[]{:S(2)}) collective-permute-start(f32[4,1,512]{2,1,0:T(1,128)S(1)} %get-tuple-element.316), channel_id=1, source_target_pairs={{1,0},{2,1},{3,2},{4,3},{5,4},{6,5},{7,6},{8,7},{9,8},{10,9},{11,1... | collective-permute-start | bytes 24584 | tf_op jit(solution)/shard_map/ppermute | solution.py:22
  31.8 1.3 collective-permute-done.3
  34.0 2.9 %collective-permute-start.4 = (f32[4,1,512]{2,1,0:T(1,128)S(1)}, f32[4,1,512]{2,1,0:T(1,128)S(1)}, u32[]{:S(2)}, u32[]{:S(2)}) collective-permute-start(f32[4,1,512]{2,1,0:T(1,128)S(1)} %get-tuple-element.306), channel_id=1, source_target_pairs={{0,1},{1,2},{2,3},{3,4},{4,5},{5,6},{6,7},{7,8},{8,9},{9,10},{10,1... | collective-permute-start | bytes 24584 | tf_op jit(solution)/shard_map/ppermute | solution.py:20
  36.8 5.4 %collective-permute-start.5 = (f32[4,1,512]{2,1,0:T(1,128)S(1)}, f32[4,1,512]{2,1,0:T(1,128)S(1)}, u32[]{:S(2)}, u32[]{:S(2)}) collective-permute-start(f32[4,1,512]{2,1,0:T(1,128)S(1)} %get-tuple-element.307), channel_id=1, source_target_pairs={{1,0},{2,1},{3,2},{4,3},{5,4},{6,5},{7,6},{8,7},{9,8},{10,9},{11,1... | collective-permute-start | bytes 24584 | tf_op jit(solution)/shard_map/ppermute | solution.py:22
  42.3 1.3 collective-permute-done.5
  44.5 3.4 %collective-permute-start.6 = (f32[4,1,512]{2,1,0:T(1,128)S(1)}, f32[4,1,512]{2,1,0:T(1,128)S(1)}, u32[]{:S(2)}, u32[]{:S(2)}) collective-permute-start(f32[4,1,512]{2,1,0:T(1,128)S(1)} %get-tuple-element.297), channel_id=1, source_target_pairs={{0,1},{1,2},{2,3},{3,4},{4,5},{5,6},{6,7},{7,8},{8,9},{9,10},{10,1... | collective-permute-start | bytes 24584 | tf_op jit(solution)/shard_map/ppermute | solution.py:20
  47.9 4.8 %collective-permute-start.7 = (f32[4,1,512]{2,1,0:T(1,128)S(1)}, f32[4,1,512]{2,1,0:T(1,128)S(1)}, u32[]{:S(2)}, u32[]{:S(2)}) collective-permute-start(f32[4,1,512]{2,1,0:T(1,128)S(1)} %get-tuple-element.298), channel_id=1, source_target_pairs={{1,0},{2,1},{3,2},{4,3},{5,4},{6,5},{7,6},{8,7},{9,8},{10,9},{11,1... | collective-permute-start | bytes 24584 | tf_op jit(solution)/shard_map/ppermute | solution.py:22
  52.8 1.3 collective-permute-done.7
  54.9 3.3 %collective-permute-start.8 = (f32[4,1,512]{2,1,0:T(1,128)S(1)}, f32[4,1,512]{2,1,0:T(1,128)S(1)}, u32[]{:S(2)}, u32[]{:S(2)}) collective-permute-start(f32[4,1,512]{2,1,0:T(1,128)S(1)} %get-tuple-element.288), channel_id=1, source_target_pairs={{0,1},{1,2},{2,3},{3,4},{4,5},{5,6},{6,7},{7,8},{8,9},{9,10},{10,1... | collective-permute-start | bytes 24584 | tf_op jit(solution)/shard_map/ppermute | solution.py:20
  58.2 4.9 %collective-permute-start.9 = (f32[4,1,512]{2,1,0:T(1,128)S(1)}, f32[4,1,512]{2,1,0:T(1,128)S(1)}, u32[]{:S(2)}, u32[]{:S(2)}) collective-permute-start(f32[4,1,512]{2,1,0:T(1,128)S(1)} %get-tuple-element.289), channel_id=1, source_target_pairs={{1,0},{2,1},{3,2},{4,3},{5,4},{6,5},{7,6},{8,7},{9,8},{10,9},{11,1... | collective-permute-start | bytes 24584 | tf_op jit(solution)/shard_map/ppermute | solution.py:22
  63.2 1.3 collective-permute-done.9
  65.4 2.4 collective-permute-start.10
  67.8 5.8 %collective-permute-start.11 = (f32[4,1,512]{2,1,0:T(1,128)S(1)}, f32[4,1,512]{2,1,0:T(1,128)S(1)}, u32[]{:S(2)}, u32[]{:S(2)}) collective-permute-start(f32[4,1,512]{2,1,0:T(1,128)S(1)} %get-tuple-element.280), channel_id=1, source_target_pairs={{1,0},{2,1},{3,2},{4,3},{5,4},{6,5},{7,6},{8,7},{9,8},{10,9},{11,1... | collective-permute-start | bytes 24584 | tf_op jit(solution)/shard_map/ppermute | solution.py:22
  73.7 1.3 collective-permute-done.11
  75.9 1.9 collective-permute-start.12
  77.8 6.3 %collective-permute-start.13 = (f32[4,1,512]{2,1,0:T(1,128)S(1)}, f32[4,1,512]{2,1,0:T(1,128)S(1)}, u32[]{:S(2)}, u32[]{:S(2)}) collective-permute-start(f32[4,1,512]{2,1,0:T(1,128)S(1)} %get-tuple-element.271), channel_id=1, source_target_pairs={{1,0},{2,1},{3,2},{4,3},{5,4},{6,5},{7,6},{8,7},{9,8},{10,9},{11,1... | collective-permute-start | bytes 24584 | tf_op jit(solution)/shard_map/ppermute | solution.py:22
  84.2 1.3 collective-permute-done.13
  86.3 1.9 collective-permute-start.14
  88.2 6.3 %collective-permute-start.15 = (f32[4,1,512]{2,1,0:T(1,128)S(1)}, f32[4,1,512]{2,1,0:T(1,128)S(1)}, u32[]{:S(2)}, u32[]{:S(2)}) collective-permute-start(f32[4,1,512]{2,1,0:T(1,128)S(1)} %get-tuple-element.262), channel_id=1, source_target_pairs={{1,0},{2,1},{3,2},{4,3},{5,4},{6,5},{7,6},{8,7},{9,8},{10,9},{11,1... | collective-permute-start | bytes 24584 | tf_op jit(solution)/shard_map/ppermute | solution.py:22
  94.6 1.3 collective-permute-done.15
  96.8 1.9 collective-permute-start.16
  98.7 6.4 %collective-permute-start.17 = (f32[4,1,512]{2,1,0:T(1,128)S(1)}, f32[4,1,512]{2,1,0:T(1,128)S(1)}, u32[]{:S(2)}, u32[]{:S(2)}) collective-permute-start(f32[4,1,512]{2,1,0:T(1,128)S(1)} %get-tuple-element.253), channel_id=1, source_target_pairs={{1,0},{2,1},{3,2},{4,3},{5,4},{6,5},{7,6},{8,7},{9,8},{10,9},{11,1... | collective-permute-start | bytes 24584 | tf_op jit(solution)/shard_map/ppermute | solution.py:22
  105.2 1.3 collective-permute-done.17
  107.1 1.1 fusion.34
  111.5 35.7 %psum.7 = f32[]{:T(128)} all-reduce(f32[]{:T(128)} %fusion.150), channel_id=1, replica_groups=mesh['member'=16,'domain'=16] {'domain'}, use_global_device_ids=true, to_apply=%region_1.2 | all-reduce | flops 1 | bytes 8 | tf_op jit(solution)/shard_map/psum | solution.py:91
  147.9 19.7 %all-gather.2.cloned.1.call-done = f32[16,4,32,512]{3,2,1,0:T(8,128)} async-done(((f32[1,4,32,512]{3,2,1,0:T(8,128)}), f32[16,4,32,512]{3,2,1,0:T(8,128)}) %all-gather.2.cloned.1.call-update) | async-done | bytes 4194320 | tf_op jit(solution)/shard_map/all_gather | solution.py:93
  167.5 1.0 select_add_fusion
  168.7 3.5 %collective-permute-start.18 = (f32[4,1,512]{2,1,0:T(1,128)S(1)}, f32[4,1,512]{2,1,0:T(1,128)S(1)}, u32[]{:S(2)}, u32[]{:S(2)}) collective-permute-start(f32[4,1,512]{2,1,0:T(1,128)S(1)} %get-tuple-element.243), channel_id=1, source_target_pairs={{0,1},{1,2},{2,3},{3,4},{4,5},{5,6},{6,7},{7,8},{8,9},{9,10},{10,1... | collective-permute-start | bytes 24584 | tf_op jit(solution)/shard_map/ppermute | solution.py:20
  172.2 4.6 %collective-permute-start.19 = (f32[4,1,512]{2,1,0:T(1,128)S(1)}, f32[4,1,512]{2,1,0:T(1,128)S(1)}, u32[]{:S(2)}, u32[]{:S(2)}) collective-permute-start(f32[4,1,512]{2,1,0:T(1,128)S(1)} %get-tuple-element.244), channel_id=1, source_target_pairs={{1,0},{2,1},{3,2},{4,3},{5,4},{6,5},{7,6},{8,7},{9,8},{10,9},{11,1... | collective-permute-start | bytes 24584 | tf_op jit(solution)/shard_map/ppermute | solution.py:22
  176.9 1.3 collective-permute-done.19
  179.0 3.1 %collective-permute-start.20 = (f32[4,1,512]{2,1,0:T(1,128)S(1)}, f32[4,1,512]{2,1,0:T(1,128)S(1)}, u32[]{:S(2)}, u32[]{:S(2)}) collective-permute-start(f32[4,1,512]{2,1,0:T(1,128)S(1)} %get-tuple-element.234), channel_id=1, source_target_pairs={{0,1},{1,2},{2,3},{3,4},{4,5},{5,6},{6,7},{7,8},{8,9},{9,10},{10,1... | collective-permute-start | bytes 24584 | tf_op jit(solution)/shard_map/ppermute | solution.py:20
  182.0 5.1 %collective-permute-start.21 = (f32[4,1,512]{2,1,0:T(1,128)S(1)}, f32[4,1,512]{2,1,0:T(1,128)S(1)}, u32[]{:S(2)}, u32[]{:S(2)}) collective-permute-start(f32[4,1,512]{2,1,0:T(1,128)S(1)} %get-tuple-element.235), channel_id=1, source_target_pairs={{1,0},{2,1},{3,2},{4,3},{5,4},{6,5},{7,6},{8,7},{9,8},{10,9},{11,1... | collective-permute-start | bytes 24584 | tf_op jit(solution)/shard_map/ppermute | solution.py:22
  187.3 1.3 collective-permute-done.21
  189.4 4.5 %collective-permute-start.22 = (f32[4,1,512]{2,1,0:T(1,128)S(1)}, f32[4,1,512]{2,1,0:T(1,128)S(1)}, u32[]{:S(2)}, u32[]{:S(2)}) collective-permute-start(f32[4,1,512]{2,1,0:T(1,128)S(1)} %get-tuple-element.225), channel_id=1, source_target_pairs={{0,1},{1,2},{2,3},{3,4},{4,5},{5,6},{6,7},{7,8},{8,9},{9,10},{10,1... | collective-permute-start | bytes 24584 | tf_op jit(solution)/shard_map/ppermute | solution.py:20
  193.9 3.7 %collective-permute-start.23 = (f32[4,1,512]{2,1,0:T(1,128)S(1)}, f32[4,1,512]{2,1,0:T(1,128)S(1)}, u32[]{:S(2)}, u32[]{:S(2)}) collective-permute-start(f32[4,1,512]{2,1,0:T(1,128)S(1)} %get-tuple-element.226), channel_id=1, source_target_pairs={{1,0},{2,1},{3,2},{4,3},{5,4},{6,5},{7,6},{8,7},{9,8},{10,9},{11,1... | collective-permute-start | bytes 24584 | tf_op jit(solution)/shard_map/ppermute | solution.py:22
  197.7 1.7 collective-permute-done.23
  200.4 3.9 %collective-permute-start.24 = (f32[4,1,512]{2,1,0:T(1,128)S(1)}, f32[4,1,512]{2,1,0:T(1,128)S(1)}, u32[]{:S(2)}, u32[]{:S(2)}) collective-permute-start(f32[4,1,512]{2,1,0:T(1,128)S(1)} %get-tuple-element.216), channel_id=1, source_target_pairs={{0,1},{1,2},{2,3},{3,4},{4,5},{5,6},{6,7},{7,8},{8,9},{9,10},{10,1... | collective-permute-start | bytes 24584 | tf_op jit(solution)/shard_map/ppermute | solution.py:20
  204.3 4.0 %collective-permute-start.25 = (f32[4,1,512]{2,1,0:T(1,128)S(1)}, f32[4,1,512]{2,1,0:T(1,128)S(1)}, u32[]{:S(2)}, u32[]{:S(2)}) collective-permute-start(f32[4,1,512]{2,1,0:T(1,128)S(1)} %get-tuple-element.217), channel_id=1, source_target_pairs={{1,0},{2,1},{3,2},{4,3},{5,4},{6,5},{7,6},{8,7},{9,8},{10,9},{11,1... | collective-permute-start | bytes 24584 | tf_op jit(solution)/shard_map/ppermute | solution.py:22
  208.4 1.4 collective-permute-done.25
  210.7 3.1 %collective-permute-start.26 = (f32[4,1,512]{2,1,0:T(1,128)S(1)}, f32[4,1,512]{2,1,0:T(1,128)S(1)}, u32[]{:S(2)}, u32[]{:S(2)}) collective-permute-start(f32[4,1,512]{2,1,0:T(1,128)S(1)} %get-tuple-element.207), channel_id=1, source_target_pairs={{0,1},{1,2},{2,3},{3,4},{4,5},{5,6},{6,7},{7,8},{8,9},{9,10},{10,1... | collective-permute-start | bytes 24584 | tf_op jit(solution)/shard_map/ppermute | solution.py:20
  213.8 5.1 %collective-permute-start.27 = (f32[4,1,512]{2,1,0:T(1,128)S(1)}, f32[4,1,512]{2,1,0:T(1,128)S(1)}, u32[]{:S(2)}, u32[]{:S(2)}) collective-permute-start(f32[4,1,512]{2,1,0:T(1,128)S(1)} %get-tuple-element.208), channel_id=1, source_target_pairs={{1,0},{2,1},{3,2},{4,3},{5,4},{6,5},{7,6},{8,7},{9,8},{10,9},{11,1... | collective-permute-start | bytes 24584 | tf_op jit(solution)/shard_map/ppermute | solution.py:22
  219.0 1.1 collective-permute-done.27
  221.0 2.4 collective-permute-start.28
  223.4 5.8 %collective-permute-start.29 = (f32[4,1,512]{2,1,0:T(1,128)S(1)}, f32[4,1,512]{2,1,0:T(1,128)S(1)}, u32[]{:S(2)}, u32[]{:S(2)}) collective-permute-start(f32[4,1,512]{2,1,0:T(1,128)S(1)} %get-tuple-element.199), channel_id=1, source_target_pairs={{1,0},{2,1},{3,2},{4,3},{5,4},{6,5},{7,6},{8,7},{9,8},{10,9},{11,1... | collective-permute-start | bytes 24584 | tf_op jit(solution)/shard_map/ppermute | solution.py:22
  229.3 1.3 collective-permute-done.29
  231.5 1.9 collective-permute-start.30
  233.4 6.3 %collective-permute-start.31 = (f32[4,1,512]{2,1,0:T(1,128)S(1)}, f32[4,1,512]{2,1,0:T(1,128)S(1)}, u32[]{:S(2)}, u32[]{:S(2)}) collective-permute-start(f32[4,1,512]{2,1,0:T(1,128)S(1)} %get-tuple-element.190), channel_id=1, source_target_pairs={{1,0},{2,1},{3,2},{4,3},{5,4},{6,5},{7,6},{8,7},{9,8},{10,9},{11,1... | collective-permute-start | bytes 24584 | tf_op jit(solution)/shard_map/ppermute | solution.py:22
  239.8 1.3 collective-permute-done.31
  241.9 1.9 collective-permute-start.32
  243.8 6.3 %collective-permute-start.33 = (f32[4,1,512]{2,1,0:T(1,128)S(1)}, f32[4,1,512]{2,1,0:T(1,128)S(1)}, u32[]{:S(2)}, u32[]{:S(2)}) collective-permute-start(f32[4,1,512]{2,1,0:T(1,128)S(1)} %get-tuple-element.181), channel_id=1, source_target_pairs={{1,0},{2,1},{3,2},{4,3},{5,4},{6,5},{7,6},{8,7},{9,8},{10,9},{11,1... | collective-permute-start | bytes 24584 | tf_op jit(solution)/shard_map/ppermute | solution.py:22
  250.2 1.3 collective-permute-done.33
  252.4 1.9 collective-permute-start.34
  254.3 6.3 %collective-permute-start.35 = (f32[4,1,512]{2,1,0:T(1,128)S(1)}, f32[4,1,512]{2,1,0:T(1,128)S(1)}, u32[]{:S(2)}, u32[]{:S(2)}) collective-permute-start(f32[4,1,512]{2,1,0:T(1,128)S(1)} %get-tuple-element.172), channel_id=1, source_target_pairs={{1,0},{2,1},{3,2},{4,3},{5,4},{6,5},{7,6},{8,7},{9,8},{10,9},{11,1... | collective-permute-start | bytes 24584 | tf_op jit(solution)/shard_map/ppermute | solution.py:22
  260.7 1.3 collective-permute-done.35
  262.6 1.1 fusion.73
  (203 shorter events, 17.0 us)
Async XLA Ops:
  7.2 16.2 %copy-start = (f32[1,4,32,512]{3,2,1,0:T(8,128)S(1)}, f32[1,4,32,512]{3,2,1,0:T(8,128)}, u32[]{:S(2)}) copy-start(f32[1,4,32,512]{3,2,1,0:T(8,128)} %param.3) | copy-start | bytes 786436
  7.2 160.4 %all-gather.2.cloned.1.call-start = ((), (), s32[]{:S(2)}) async-start(), calls=%async_computation | async-start | bytes 4456448 | tf_op jit(solution)/shard_map/all_gather | solution.py:93
  8.1 12.7 %collective-permute-start = (f32[4,1,512]{2,1,0:T(1,128)S(1)}, f32[4,1,512]{2,1,0:T(1,128)S(1)}, u32[]{:S(2)}, u32[]{:S(2)}) collective-permute-start(f32[4,1,512]{2,1,0:T(1,128)S(1)} %get-tuple-element.324), channel_id=1, source_target_pairs={{0,1},{1,2},{2,3},{3,4},{4,5},{5,6},{6,7},{7,8},{8,9},{9,10},{10,1... | collective-permute-start | bytes 24584 | tf_op jit(solution)/shard_map/ppermute | solution.py:20
  12.0 8.9 %collective-permute-start.1 = (f32[4,1,512]{2,1,0:T(1,128)S(1)}, f32[4,1,512]{2,1,0:T(1,128)S(1)}, u32[]{:S(2)}, u32[]{:S(2)}) collective-permute-start(f32[4,1,512]{2,1,0:T(1,128)S(1)} %get-tuple-element.325), channel_id=1, source_target_pairs={{1,0},{2,1},{3,2},{4,3},{5,4},{6,5},{7,6},{8,7},{9,8},{10,9},{11,1... | collective-permute-start | bytes 24584 | tf_op jit(solution)/shard_map/ppermute | solution.py:22
  23.8 8.1 %collective-permute-start.2 = (f32[4,1,512]{2,1,0:T(1,128)S(1)}, f32[4,1,512]{2,1,0:T(1,128)S(1)}, u32[]{:S(2)}, u32[]{:S(2)}) collective-permute-start(f32[4,1,512]{2,1,0:T(1,128)S(1)} %get-tuple-element.315), channel_id=1, source_target_pairs={{0,1},{1,2},{2,3},{3,4},{4,5},{5,6},{6,7},{7,8},{8,9},{9,10},{10,1... | collective-permute-start | bytes 24584 | tf_op jit(solution)/shard_map/ppermute | solution.py:20
  25.7 7.4 %collective-permute-start.3 = (f32[4,1,512]{2,1,0:T(1,128)S(1)}, f32[4,1,512]{2,1,0:T(1,128)S(1)}, u32[]{:S(2)}, u32[]{:S(2)}) collective-permute-start(f32[4,1,512]{2,1,0:T(1,128)S(1)} %get-tuple-element.316), channel_id=1, source_target_pairs={{1,0},{2,1},{3,2},{4,3},{5,4},{6,5},{7,6},{8,7},{9,8},{10,9},{11,1... | collective-permute-start | bytes 24584 | tf_op jit(solution)/shard_map/ppermute | solution.py:22
  34.0 8.3 %collective-permute-start.4 = (f32[4,1,512]{2,1,0:T(1,128)S(1)}, f32[4,1,512]{2,1,0:T(1,128)S(1)}, u32[]{:S(2)}, u32[]{:S(2)}) collective-permute-start(f32[4,1,512]{2,1,0:T(1,128)S(1)} %get-tuple-element.306), channel_id=1, source_target_pairs={{0,1},{1,2},{2,3},{3,4},{4,5},{5,6},{6,7},{7,8},{8,9},{9,10},{10,1... | collective-permute-start | bytes 24584 | tf_op jit(solution)/shard_map/ppermute | solution.py:20
  36.8 6.7 %collective-permute-start.5 = (f32[4,1,512]{2,1,0:T(1,128)S(1)}, f32[4,1,512]{2,1,0:T(1,128)S(1)}, u32[]{:S(2)}, u32[]{:S(2)}) collective-permute-start(f32[4,1,512]{2,1,0:T(1,128)S(1)} %get-tuple-element.307), channel_id=1, source_target_pairs={{1,0},{2,1},{3,2},{4,3},{5,4},{6,5},{7,6},{8,7},{9,8},{10,9},{11,1... | collective-permute-start | bytes 24584 | tf_op jit(solution)/shard_map/ppermute | solution.py:22
  44.5 8.3 %collective-permute-start.6 = (f32[4,1,512]{2,1,0:T(1,128)S(1)}, f32[4,1,512]{2,1,0:T(1,128)S(1)}, u32[]{:S(2)}, u32[]{:S(2)}) collective-permute-start(f32[4,1,512]{2,1,0:T(1,128)S(1)} %get-tuple-element.297), channel_id=1, source_target_pairs={{0,1},{1,2},{2,3},{3,4},{4,5},{5,6},{6,7},{7,8},{8,9},{9,10},{10,1... | collective-permute-start | bytes 24584 | tf_op jit(solution)/shard_map/ppermute | solution.py:20
  47.9 6.2 %collective-permute-start.7 = (f32[4,1,512]{2,1,0:T(1,128)S(1)}, f32[4,1,512]{2,1,0:T(1,128)S(1)}, u32[]{:S(2)}, u32[]{:S(2)}) collective-permute-start(f32[4,1,512]{2,1,0:T(1,128)S(1)} %get-tuple-element.298), channel_id=1, source_target_pairs={{1,0},{2,1},{3,2},{4,3},{5,4},{6,5},{7,6},{8,7},{9,8},{10,9},{11,1... | collective-permute-start | bytes 24584 | tf_op jit(solution)/shard_map/ppermute | solution.py:22
  54.9 8.3 %collective-permute-start.8 = (f32[4,1,512]{2,1,0:T(1,128)S(1)}, f32[4,1,512]{2,1,0:T(1,128)S(1)}, u32[]{:S(2)}, u32[]{:S(2)}) collective-permute-start(f32[4,1,512]{2,1,0:T(1,128)S(1)} %get-tuple-element.288), channel_id=1, source_target_pairs={{0,1},{1,2},{2,3},{3,4},{4,5},{5,6},{6,7},{7,8},{8,9},{9,10},{10,1... | collective-permute-start | bytes 24584 | tf_op jit(solution)/shard_map/ppermute | solution.py:20
  58.2 6.3 %collective-permute-start.9 = (f32[4,1,512]{2,1,0:T(1,128)S(1)}, f32[4,1,512]{2,1,0:T(1,128)S(1)}, u32[]{:S(2)}, u32[]{:S(2)}) collective-permute-start(f32[4,1,512]{2,1,0:T(1,128)S(1)} %get-tuple-element.289), channel_id=1, source_target_pairs={{1,0},{2,1},{3,2},{4,3},{5,4},{6,5},{7,6},{8,7},{9,8},{10,9},{11,1... | collective-permute-start | bytes 24584 | tf_op jit(solution)/shard_map/ppermute | solution.py:22
  65.4 8.3 %collective-permute-start.10 = (f32[4,1,512]{2,1,0:T(1,128)S(1)}, f32[4,1,512]{2,1,0:T(1,128)S(1)}, u32[]{:S(2)}, u32[]{:S(2)}) collective-permute-start(f32[4,1,512]{2,1,0:T(1,128)S(1)} %get-tuple-element.279), channel_id=1, source_target_pairs={{0,1},{1,2},{2,3},{3,4},{4,5},{5,6},{6,7},{7,8},{8,9},{9,10},{10,1... | collective-permute-start | bytes 24584 | tf_op jit(solution)/shard_map/ppermute | solution.py:20
  67.8 7.2 %collective-permute-start.11 = (f32[4,1,512]{2,1,0:T(1,128)S(1)}, f32[4,1,512]{2,1,0:T(1,128)S(1)}, u32[]{:S(2)}, u32[]{:S(2)}) collective-permute-start(f32[4,1,512]{2,1,0:T(1,128)S(1)} %get-tuple-element.280), channel_id=1, source_target_pairs={{1,0},{2,1},{3,2},{4,3},{5,4},{6,5},{7,6},{8,7},{9,8},{10,9},{11,1... | collective-permute-start | bytes 24584 | tf_op jit(solution)/shard_map/ppermute | solution.py:22
  75.9 8.3 %collective-permute-start.12 = (f32[4,1,512]{2,1,0:T(1,128)S(1)}, f32[4,1,512]{2,1,0:T(1,128)S(1)}, u32[]{:S(2)}, u32[]{:S(2)}) collective-permute-start(f32[4,1,512]{2,1,0:T(1,128)S(1)} %get-tuple-element.270), channel_id=1, source_target_pairs={{0,1},{1,2},{2,3},{3,4},{4,5},{5,6},{6,7},{7,8},{8,9},{9,10},{10,1... | collective-permute-start | bytes 24584 | tf_op jit(solution)/shard_map/ppermute | solution.py:20
  77.8 7.7 %collective-permute-start.13 = (f32[4,1,512]{2,1,0:T(1,128)S(1)}, f32[4,1,512]{2,1,0:T(1,128)S(1)}, u32[]{:S(2)}, u32[]{:S(2)}) collective-permute-start(f32[4,1,512]{2,1,0:T(1,128)S(1)} %get-tuple-element.271), channel_id=1, source_target_pairs={{1,0},{2,1},{3,2},{4,3},{5,4},{6,5},{7,6},{8,7},{9,8},{10,9},{11,1... | collective-permute-start | bytes 24584 | tf_op jit(solution)/shard_map/ppermute | solution.py:22
  86.3 8.3 %collective-permute-start.14 = (f32[4,1,512]{2,1,0:T(1,128)S(1)}, f32[4,1,512]{2,1,0:T(1,128)S(1)}, u32[]{:S(2)}, u32[]{:S(2)}) collective-permute-start(f32[4,1,512]{2,1,0:T(1,128)S(1)} %get-tuple-element.261), channel_id=1, source_target_pairs={{0,1},{1,2},{2,3},{3,4},{4,5},{5,6},{6,7},{7,8},{8,9},{9,10},{10,1... | collective-permute-start | bytes 24584 | tf_op jit(solution)/shard_map/ppermute | solution.py:20
  88.2 7.7 %collective-permute-start.15 = (f32[4,1,512]{2,1,0:T(1,128)S(1)}, f32[4,1,512]{2,1,0:T(1,128)S(1)}, u32[]{:S(2)}, u32[]{:S(2)}) collective-permute-start(f32[4,1,512]{2,1,0:T(1,128)S(1)} %get-tuple-element.262), channel_id=1, source_target_pairs={{1,0},{2,1},{3,2},{4,3},{5,4},{6,5},{7,6},{8,7},{9,8},{10,9},{11,1... | collective-permute-start | bytes 24584 | tf_op jit(solution)/shard_map/ppermute | solution.py:22
  96.7 11.5 %copy-start.2 = (s32[16]{0:T(128)S(1)}, s32[16]{0:T(128)}, u32[]{:S(2)}) copy-start(s32[16]{0:T(128)} %param.5) | copy-start | bytes 196
  96.8 8.5 %collective-permute-start.16 = (f32[4,1,512]{2,1,0:T(1,128)S(1)}, f32[4,1,512]{2,1,0:T(1,128)S(1)}, u32[]{:S(2)}, u32[]{:S(2)}) collective-permute-start(f32[4,1,512]{2,1,0:T(1,128)S(1)} %get-tuple-element.252), channel_id=1, source_target_pairs={{0,1},{1,2},{2,3},{3,4},{4,5},{5,6},{6,7},{7,8},{8,9},{9,10},{10,1... | collective-permute-start | bytes 24584 | tf_op jit(solution)/shard_map/ppermute | solution.py:20
  98.7 68.8 %copy-start.1 = (f32[1,4,32,512]{3,2,1,0:T(8,128)S(1)}, f32[1,4,32,512]{3,2,1,0:T(8,128)}, u32[]{:S(2)}) copy-start(f32[1,4,32,512]{3,2,1,0:T(8,128)} %param.4) | copy-start | bytes 786436
  98.7 7.8 %collective-permute-start.17 = (f32[4,1,512]{2,1,0:T(1,128)S(1)}, f32[4,1,512]{2,1,0:T(1,128)S(1)}, u32[]{:S(2)}, u32[]{:S(2)}) collective-permute-start(f32[4,1,512]{2,1,0:T(1,128)S(1)} %get-tuple-element.253), channel_id=1, source_target_pairs={{1,0},{2,1},{3,2},{4,3},{5,4},{6,5},{7,6},{8,7},{9,8},{10,9},{11,1... | collective-permute-start | bytes 24584 | tf_op jit(solution)/shard_map/ppermute | solution.py:22
  168.7 8.1 %collective-permute-start.18 = (f32[4,1,512]{2,1,0:T(1,128)S(1)}, f32[4,1,512]{2,1,0:T(1,128)S(1)}, u32[]{:S(2)}, u32[]{:S(2)}) collective-permute-start(f32[4,1,512]{2,1,0:T(1,128)S(1)} %get-tuple-element.243), channel_id=1, source_target_pairs={{0,1},{1,2},{2,3},{3,4},{4,5},{5,6},{6,7},{7,8},{8,9},{9,10},{10,1... | collective-permute-start | bytes 24584 | tf_op jit(solution)/shard_map/ppermute | solution.py:20
  172.2 5.9 %collective-permute-start.19 = (f32[4,1,512]{2,1,0:T(1,128)S(1)}, f32[4,1,512]{2,1,0:T(1,128)S(1)}, u32[]{:S(2)}, u32[]{:S(2)}) collective-permute-start(f32[4,1,512]{2,1,0:T(1,128)S(1)} %get-tuple-element.244), channel_id=1, source_target_pairs={{1,0},{2,1},{3,2},{4,3},{5,4},{6,5},{7,6},{8,7},{9,8},{10,9},{11,1... | collective-permute-start | bytes 24584 | tf_op jit(solution)/shard_map/ppermute | solution.py:22
  179.0 8.3 %collective-permute-start.20 = (f32[4,1,512]{2,1,0:T(1,128)S(1)}, f32[4,1,512]{2,1,0:T(1,128)S(1)}, u32[]{:S(2)}, u32[]{:S(2)}) collective-permute-start(f32[4,1,512]{2,1,0:T(1,128)S(1)} %get-tuple-element.234), channel_id=1, source_target_pairs={{0,1},{1,2},{2,3},{3,4},{4,5},{5,6},{6,7},{7,8},{8,9},{9,10},{10,1... | collective-permute-start | bytes 24584 | tf_op jit(solution)/shard_map/ppermute | solution.py:20
  182.0 6.5 %collective-permute-start.21 = (f32[4,1,512]{2,1,0:T(1,128)S(1)}, f32[4,1,512]{2,1,0:T(1,128)S(1)}, u32[]{:S(2)}, u32[]{:S(2)}) collective-permute-start(f32[4,1,512]{2,1,0:T(1,128)S(1)} %get-tuple-element.235), channel_id=1, source_target_pairs={{1,0},{2,1},{3,2},{4,3},{5,4},{6,5},{7,6},{8,7},{9,8},{10,9},{11,1... | collective-permute-start | bytes 24584 | tf_op jit(solution)/shard_map/ppermute | solution.py:22
  189.4 8.3 %collective-permute-start.22 = (f32[4,1,512]{2,1,0:T(1,128)S(1)}, f32[4,1,512]{2,1,0:T(1,128)S(1)}, u32[]{:S(2)}, u32[]{:S(2)}) collective-permute-start(f32[4,1,512]{2,1,0:T(1,128)S(1)} %get-tuple-element.225), channel_id=1, source_target_pairs={{0,1},{1,2},{2,3},{3,4},{4,5},{5,6},{6,7},{7,8},{8,9},{9,10},{10,1... | collective-permute-start | bytes 24584 | tf_op jit(solution)/shard_map/ppermute | solution.py:20
  193.9 5.5 %collective-permute-start.23 = (f32[4,1,512]{2,1,0:T(1,128)S(1)}, f32[4,1,512]{2,1,0:T(1,128)S(1)}, u32[]{:S(2)}, u32[]{:S(2)}) collective-permute-start(f32[4,1,512]{2,1,0:T(1,128)S(1)} %get-tuple-element.226), channel_id=1, source_target_pairs={{1,0},{2,1},{3,2},{4,3},{5,4},{6,5},{7,6},{8,7},{9,8},{10,9},{11,1... | collective-permute-start | bytes 24584 | tf_op jit(solution)/shard_map/ppermute | solution.py:22
  200.4 8.1 %collective-permute-start.24 = (f32[4,1,512]{2,1,0:T(1,128)S(1)}, f32[4,1,512]{2,1,0:T(1,128)S(1)}, u32[]{:S(2)}, u32[]{:S(2)}) collective-permute-start(f32[4,1,512]{2,1,0:T(1,128)S(1)} %get-tuple-element.216), channel_id=1, source_target_pairs={{0,1},{1,2},{2,3},{3,4},{4,5},{5,6},{6,7},{7,8},{8,9},{9,10},{10,1... | collective-permute-start | bytes 24584 | tf_op jit(solution)/shard_map/ppermute | solution.py:20
  204.3 5.5 %collective-permute-start.25 = (f32[4,1,512]{2,1,0:T(1,128)S(1)}, f32[4,1,512]{2,1,0:T(1,128)S(1)}, u32[]{:S(2)}, u32[]{:S(2)}) collective-permute-start(f32[4,1,512]{2,1,0:T(1,128)S(1)} %get-tuple-element.217), channel_id=1, source_target_pairs={{1,0},{2,1},{3,2},{4,3},{5,4},{6,5},{7,6},{8,7},{9,8},{10,9},{11,1... | collective-permute-start | bytes 24584 | tf_op jit(solution)/shard_map/ppermute | solution.py:22
  210.7 8.3 %collective-permute-start.26 = (f32[4,1,512]{2,1,0:T(1,128)S(1)}, f32[4,1,512]{2,1,0:T(1,128)S(1)}, u32[]{:S(2)}, u32[]{:S(2)}) collective-permute-start(f32[4,1,512]{2,1,0:T(1,128)S(1)} %get-tuple-element.207), channel_id=1, source_target_pairs={{0,1},{1,2},{2,3},{3,4},{4,5},{5,6},{6,7},{7,8},{8,9},{9,10},{10,1... | collective-permute-start | bytes 24584 | tf_op jit(solution)/shard_map/ppermute | solution.py:20
  213.8 6.3 %collective-permute-start.27 = (f32[4,1,512]{2,1,0:T(1,128)S(1)}, f32[4,1,512]{2,1,0:T(1,128)S(1)}, u32[]{:S(2)}, u32[]{:S(2)}) collective-permute-start(f32[4,1,512]{2,1,0:T(1,128)S(1)} %get-tuple-element.208), channel_id=1, source_target_pairs={{1,0},{2,1},{3,2},{4,3},{5,4},{6,5},{7,6},{8,7},{9,8},{10,9},{11,1... | collective-permute-start | bytes 24584 | tf_op jit(solution)/shard_map/ppermute | solution.py:22
  221.0 8.3 %collective-permute-start.28 = (f32[4,1,512]{2,1,0:T(1,128)S(1)}, f32[4,1,512]{2,1,0:T(1,128)S(1)}, u32[]{:S(2)}, u32[]{:S(2)}) collective-permute-start(f32[4,1,512]{2,1,0:T(1,128)S(1)} %get-tuple-element.198), channel_id=1, source_target_pairs={{0,1},{1,2},{2,3},{3,4},{4,5},{5,6},{6,7},{7,8},{8,9},{9,10},{10,1... | collective-permute-start | bytes 24584 | tf_op jit(solution)/shard_map/ppermute | solution.py:20
  223.4 7.2 %collective-permute-start.29 = (f32[4,1,512]{2,1,0:T(1,128)S(1)}, f32[4,1,512]{2,1,0:T(1,128)S(1)}, u32[]{:S(2)}, u32[]{:S(2)}) collective-permute-start(f32[4,1,512]{2,1,0:T(1,128)S(1)} %get-tuple-element.199), channel_id=1, source_target_pairs={{1,0},{2,1},{3,2},{4,3},{5,4},{6,5},{7,6},{8,7},{9,8},{10,9},{11,1... | collective-permute-start | bytes 24584 | tf_op jit(solution)/shard_map/ppermute | solution.py:22
  231.5 8.3 %collective-permute-start.30 = (f32[4,1,512]{2,1,0:T(1,128)S(1)}, f32[4,1,512]{2,1,0:T(1,128)S(1)}, u32[]{:S(2)}, u32[]{:S(2)}) collective-permute-start(f32[4,1,512]{2,1,0:T(1,128)S(1)} %get-tuple-element.189), channel_id=1, source_target_pairs={{0,1},{1,2},{2,3},{3,4},{4,5},{5,6},{6,7},{7,8},{8,9},{9,10},{10,1... | collective-permute-start | bytes 24584 | tf_op jit(solution)/shard_map/ppermute | solution.py:20
  233.4 7.7 %collective-permute-start.31 = (f32[4,1,512]{2,1,0:T(1,128)S(1)}, f32[4,1,512]{2,1,0:T(1,128)S(1)}, u32[]{:S(2)}, u32[]{:S(2)}) collective-permute-start(f32[4,1,512]{2,1,0:T(1,128)S(1)} %get-tuple-element.190), channel_id=1, source_target_pairs={{1,0},{2,1},{3,2},{4,3},{5,4},{6,5},{7,6},{8,7},{9,8},{10,9},{11,1... | collective-permute-start | bytes 24584 | tf_op jit(solution)/shard_map/ppermute | solution.py:22
  241.9 8.3 %collective-permute-start.32 = (f32[4,1,512]{2,1,0:T(1,128)S(1)}, f32[4,1,512]{2,1,0:T(1,128)S(1)}, u32[]{:S(2)}, u32[]{:S(2)}) collective-permute-start(f32[4,1,512]{2,1,0:T(1,128)S(1)} %get-tuple-element.180), channel_id=1, source_target_pairs={{0,1},{1,2},{2,3},{3,4},{4,5},{5,6},{6,7},{7,8},{8,9},{9,10},{10,1... | collective-permute-start | bytes 24584 | tf_op jit(solution)/shard_map/ppermute | solution.py:20
  243.8 7.7 %collective-permute-start.33 = (f32[4,1,512]{2,1,0:T(1,128)S(1)}, f32[4,1,512]{2,1,0:T(1,128)S(1)}, u32[]{:S(2)}, u32[]{:S(2)}) collective-permute-start(f32[4,1,512]{2,1,0:T(1,128)S(1)} %get-tuple-element.181), channel_id=1, source_target_pairs={{1,0},{2,1},{3,2},{4,3},{5,4},{6,5},{7,6},{8,7},{9,8},{10,9},{11,1... | collective-permute-start | bytes 24584 | tf_op jit(solution)/shard_map/ppermute | solution.py:22
  252.4 8.3 %collective-permute-start.34 = (f32[4,1,512]{2,1,0:T(1,128)S(1)}, f32[4,1,512]{2,1,0:T(1,128)S(1)}, u32[]{:S(2)}, u32[]{:S(2)}) collective-permute-start(f32[4,1,512]{2,1,0:T(1,128)S(1)} %get-tuple-element.171), channel_id=1, source_target_pairs={{0,1},{1,2},{2,3},{3,4},{4,5},{5,6},{6,7},{7,8},{8,9},{9,10},{10,1... | collective-permute-start | bytes 24584 | tf_op jit(solution)/shard_map/ppermute | solution.py:20
  254.3 7.7 %collective-permute-start.35 = (f32[4,1,512]{2,1,0:T(1,128)S(1)}, f32[4,1,512]{2,1,0:T(1,128)S(1)}, u32[]{:S(2)}, u32[]{:S(2)}) collective-permute-start(f32[4,1,512]{2,1,0:T(1,128)S(1)} %get-tuple-element.172), channel_id=1, source_target_pairs={{1,0},{2,1},{3,2},{4,3},{5,4},{6,5},{7,6},{8,7},{9,8},{10,9},{11,1... | collective-permute-start | bytes 24584 | tf_op jit(solution)/shard_map/ppermute | solution.py:22
Sparse Core Ops, SparseCore 0:
  108.4 59.1 all-gather.1
where the time goes:
time: 273 us; the launch traced here: 272 us
  starting transfers between devices  149 us (55%)
  waiting for transfers between devices  41.5 us (15%)
  blocking collectives  35.7 us (13%)
  between operations  19.1 us (7%)
  other arithmetic  18.9 us (7%)
  local copies, waits for them, and re-layouts  7.54 us (3%)
    ppermute x18, starting transfers between devices, with_halo(): lax.ppermute(head, axis, [((i + 1) % count, i) for i in range(ends)])  99.1 us
    ppermute x18, starting transfers between devices, with_halo(): lax.ppermute(tail, axis, [(i, (i + 1) % count) for i in range(ends)])  49.7 us
    psum x1, blocking collectives, on_device(): score = lax.psum(local_score, 'domain') / (total_rows * width)  35.7 us
    ppermute x18, waiting for transfers between devices, with_halo(): lax.ppermute(head, axis, [((i + 1) % count, i) for i in range(ends)])  21.8 us
    all_gather x1, waiting for transfers between devices, on_device(): piece = lax.all_gather(before[None], 'member', axis=0, tiled=True)  19.7 us
    slice x36, local copies, waits for them, and re-layouts, gradients(): east = jnp.roll(middle, -1, axis=-1)  5.76 us
    add x18, other arithmetic, tendency(): advect = speed_u * grad_x + speed_v * grad_y  5.57 us
  transfers between devices with their start and end apart: 37, of which 18 were waited for; matrix products, arithmetic and copies ran while one was open for 2% of the time, Pallas kernels for 0%

commit v1 on v0

--- a/solution.py
+++ b/solution.py
@@ -90,7 +90,9 @@
     local_score = jnp.sum(weight[:, None] * before[3] * before[3])
     score = lax.psum(local_score, "domain") / (total_rows * width)
     parent = lax.dynamic_index_in_dim(parents, lax.axis_index("member"), 0, keepdims=False)
-    piece = lax.all_gather(before[None], "member", axis=0, tiled=True)
+    piece = jnp.concatenate(
+        lax.all_to_all(jnp.stack([before[None]] * lax.axis_size("member")), "member", 0, 0), axis=0
+    )
     count = piece.shape[0]
     inside = (parent >= 0) & (parent < count)
     chosen = lax.dynamic_index_in_dim(piece, jnp.clip(parent, 0, count - 1), 0, keepdims=False)

time: 273 us -> 263 us (0.963)
  between operations: 19.1 us -> 5.71 us
  waiting for transfers between devices: 41.5 us -> 33 us
  starting transfers between devices: 149 us -> 157 us
    all_gather x1 -> x0, waiting for transfers between devices: 19.7 us -> none  [on_device(): piece = lax.all_gather(before[None], 'member', axis=0, tiled=True)]
    all_to_all x0 -> x1, waiting for transfers between devices: none -> 11.6 us  [on_device(): lax.all_to_all(jnp.stack([before[None]] * lax.axis_size('member')), 'memb...]
    ppermute x18, starting transfers between devices: 99.1 us -> 109 us  [with_halo(): lax.ppermute(head, axis, [((i + 1) % count, i) for i in range(ends)])]
    ppermute x18, starting transfers between devices: 49.7 us -> 40.8 us  [with_halo(): lax.ppermute(tail, axis, [(i, (i + 1) % count) for i in range(ends)])]
    all_to_all x0 -> x1, starting transfers between devices: none -> 6.61 us  [on_device(): lax.all_to_all(jnp.stack([before[None]] * lax.axis_size('member')), 'memb...]
where the time goes in v1:
time: 263 us; the launch traced here: 261 us
  starting transfers between devices  157 us (60%)
  blocking collectives  36.9 us (14%)
  waiting for transfers between devices  33 us (13%)
  other arithmetic  18.9 us (7%)
  local copies, waits for them, and re-layouts  10.2 us (4%)
  between operations  5.71 us (2%)
    ppermute x18, starting transfers between devices, with_halo(): lax.ppermute(head, axis, [((i + 1) % count, i) for i in range(ends)])  109 us
    ppermute x18, starting transfers between devices, with_halo(): lax.ppermute(tail, axis, [(i, (i + 1) % count) for i in range(ends)])  40.8 us
    psum x1, blocking collectives, on_device(): score = lax.psum(local_score, 'domain') / (total_rows * width)  36.9 us
    ppermute x18, waiting for transfers between devices, with_halo(): lax.ppermute(head, axis, [((i + 1) % count, i) for i in range(ends)])  21.4 us
    all_to_all x1, waiting for transfers between devices, on_device(): lax.all_to_all(jnp.stack([before[None]] * lax.axis_size('member')), 'memb...  11.6 us
    all_to_all x1, starting transfers between devices, on_device(): lax.all_to_all(jnp.stack([before[None]] * lax.axis_size('member')), 'memb...  6.61 us
    slice x36, local copies, waits for them, and re-layouts, gradients(): east = jnp.roll(middle, -1, axis=-1)  5.77 us
    add x18, other arithmetic, tendency(): advect = speed_u * grad_x + speed_v * grad_y  5.5 us
  transfers between devices with their start and end apart: 37, of which 18 were waited for; matrix products, arithmetic and copies ran while one was open for 2% of the time, Pallas kernels for 0%

profile of v1, /device:TPU:2, one launch (start us, length us, event | category | flops | bytes accessed | tf_op | source)
XLA Modules:
  0.0 261.4 jit_solution(2963188655079253780)
XLA Ops:
  0.6 0.9 fusion.505
  1.6 3.8 %collective-permute-start = (f32[4,1,512]{2,1,0:T(1,128)S(1)}, f32[4,1,512]{2,1,0:T(1,128)S(1)}, u32[]{:S(2)}, u32[]{:S(2)}) collective-permute-start(f32[4,1,512]{2,1,0:T(1,128)S(1)} %get-tuple-element.324), channel_id=1, source_target_pairs={{0,1},{1,2},{2,3},{3,4},{4,5},{5,6},{6,7},{7,8},{8,9},{9,10},{10,1... | collective-permute-start | bytes 24584 | tf_op jit(solution)/shard_map/ppermute | solution.py:20
  5.4 5.8 %collective-permute-start.1 = (f32[4,1,512]{2,1,0:T(1,128)S(1)}, f32[4,1,512]{2,1,0:T(1,128)S(1)}, u32[]{:S(2)}, u32[]{:S(2)}) collective-permute-start(f32[4,1,512]{2,1,0:T(1,128)S(1)} %get-tuple-element.325), channel_id=1, source_target_pairs={{1,0},{2,1},{3,2},{4,3},{5,4},{6,5},{7,6},{8,7},{9,8},{10,9},{11,1... | collective-permute-start | bytes 24584 | tf_op jit(solution)/shard_map/ppermute | solution.py:22
  11.2 1.0 fusion.504
  13.1 1.2 fusion.503
  14.3 0.9 maximum_multiply_fusion.51
  15.4 1.4 multiply_add_fusion.17
  17.2 1.9 collective-permute-start.2
  19.2 6.0 %collective-permute-start.3 = (f32[4,1,512]{2,1,0:T(1,128)S(1)}, f32[4,1,512]{2,1,0:T(1,128)S(1)}, u32[]{:S(2)}, u32[]{:S(2)}) collective-permute-start(f32[4,1,512]{2,1,0:T(1,128)S(1)} %get-tuple-element.316), channel_id=1, source_target_pairs={{1,0},{2,1},{3,2},{4,3},{5,4},{6,5},{7,6},{8,7},{9,8},{10,9},{11,1... | collective-permute-start | bytes 24584 | tf_op jit(solution)/shard_map/ppermute | solution.py:22
  25.3 1.3 collective-permute-done.3
  27.4 2.9 %collective-permute-start.4 = (f32[4,1,512]{2,1,0:T(1,128)S(1)}, f32[4,1,512]{2,1,0:T(1,128)S(1)}, u32[]{:S(2)}, u32[]{:S(2)}) collective-permute-start(f32[4,1,512]{2,1,0:T(1,128)S(1)} %get-tuple-element.306), channel_id=1, source_target_pairs={{0,1},{1,2},{2,3},{3,4},{4,5},{5,6},{6,7},{7,8},{8,9},{9,10},{10,1... | collective-permute-start | bytes 24584 | tf_op jit(solution)/shard_map/ppermute | solution.py:20
  30.3 5.4 %collective-permute-start.5 = (f32[4,1,512]{2,1,0:T(1,128)S(1)}, f32[4,1,512]{2,1,0:T(1,128)S(1)}, u32[]{:S(2)}, u32[]{:S(2)}) collective-permute-start(f32[4,1,512]{2,1,0:T(1,128)S(1)} %get-tuple-element.307), channel_id=1, source_target_pairs={{1,0},{2,1},{3,2},{4,3},{5,4},{6,5},{7,6},{8,7},{9,8},{10,9},{11,1... | collective-permute-start | bytes 24584 | tf_op jit(solution)/shard_map/ppermute | solution.py:22
  35.8 1.3 collective-permute-done.5
  38.0 3.4 %collective-permute-start.6 = (f32[4,1,512]{2,1,0:T(1,128)S(1)}, f32[4,1,512]{2,1,0:T(1,128)S(1)}, u32[]{:S(2)}, u32[]{:S(2)}) collective-permute-start(f32[4,1,512]{2,1,0:T(1,128)S(1)} %get-tuple-element.297), channel_id=1, source_target_pairs={{0,1},{1,2},{2,3},{3,4},{4,5},{5,6},{6,7},{7,8},{8,9},{9,10},{10,1... | collective-permute-start | bytes 24584 | tf_op jit(solution)/shard_map/ppermute | solution.py:20
  41.4 4.8 %collective-permute-start.7 = (f32[4,1,512]{2,1,0:T(1,128)S(1)}, f32[4,1,512]{2,1,0:T(1,128)S(1)}, u32[]{:S(2)}, u32[]{:S(2)}) collective-permute-start(f32[4,1,512]{2,1,0:T(1,128)S(1)} %get-tuple-element.298), channel_id=1, source_target_pairs={{1,0},{2,1},{3,2},{4,3},{5,4},{6,5},{7,6},{8,7},{9,8},{10,9},{11,1... | collective-permute-start | bytes 24584 | tf_op jit(solution)/shard_map/ppermute | solution.py:22
  46.3 1.3 collective-permute-done.7
  48.4 3.3 %collective-permute-start.8 = (f32[4,1,512]{2,1,0:T(1,128)S(1)}, f32[4,1,512]{2,1,0:T(1,128)S(1)}, u32[]{:S(2)}, u32[]{:S(2)}) collective-permute-start(f32[4,1,512]{2,1,0:T(1,128)S(1)} %get-tuple-element.288), channel_id=1, source_target_pairs={{0,1},{1,2},{2,3},{3,4},{4,5},{5,6},{6,7},{7,8},{8,9},{9,10},{10,1... | collective-permute-start | bytes 24584 | tf_op jit(solution)/shard_map/ppermute | solution.py:20
  51.7 4.9 %collective-permute-start.9 = (f32[4,1,512]{2,1,0:T(1,128)S(1)}, f32[4,1,512]{2,1,0:T(1,128)S(1)}, u32[]{:S(2)}, u32[]{:S(2)}) collective-permute-start(f32[4,1,512]{2,1,0:T(1,128)S(1)} %get-tuple-element.289), channel_id=1, source_target_pairs={{1,0},{2,1},{3,2},{4,3},{5,4},{6,5},{7,6},{8,7},{9,8},{10,9},{11,1... | collective-permute-start | bytes 24584 | tf_op jit(solution)/shard_map/ppermute | solution.py:22
  56.7 1.3 collective-permute-done.9
  58.8 2.4 collective-permute-start.10
  61.3 5.8 %collective-permute-start.11 = (f32[4,1,512]{2,1,0:T(1,128)S(1)}, f32[4,1,512]{2,1,0:T(1,128)S(1)}, u32[]{:S(2)}, u32[]{:S(2)}) collective-permute-start(f32[4,1,512]{2,1,0:T(1,128)S(1)} %get-tuple-element.280), channel_id=1, source_target_pairs={{1,0},{2,1},{3,2},{4,3},{5,4},{6,5},{7,6},{8,7},{9,8},{10,9},{11,1... | collective-permute-start | bytes 24584 | tf_op jit(solution)/shard_map/ppermute | solution.py:22
  67.2 1.3 collective-permute-done.11
  69.4 1.9 collective-permute-start.12
  71.3 6.3 %collective-permute-start.13 = (f32[4,1,512]{2,1,0:T(1,128)S(1)}, f32[4,1,512]{2,1,0:T(1,128)S(1)}, u32[]{:S(2)}, u32[]{:S(2)}) collective-permute-start(f32[4,1,512]{2,1,0:T(1,128)S(1)} %get-tuple-element.271), channel_id=1, source_target_pairs={{1,0},{2,1},{3,2},{4,3},{5,4},{6,5},{7,6},{8,7},{9,8},{10,9},{11,1... | collective-permute-start | bytes 24584 | tf_op jit(solution)/shard_map/ppermute | solution.py:22
  77.7 1.3 collective-permute-done.13
  79.8 1.9 collective-permute-start.14
  81.7 6.3 %collective-permute-start.15 = (f32[4,1,512]{2,1,0:T(1,128)S(1)}, f32[4,1,512]{2,1,0:T(1,128)S(1)}, u32[]{:S(2)}, u32[]{:S(2)}) collective-permute-start(f32[4,1,512]{2,1,0:T(1,128)S(1)} %get-tuple-element.262), channel_id=1, source_target_pairs={{1,0},{2,1},{3,2},{4,3},{5,4},{6,5},{7,6},{8,7},{9,8},{10,9},{11,1... | collective-permute-start | bytes 24584 | tf_op jit(solution)/shard_map/ppermute | solution.py:22
  88.1 1.3 collective-permute-done.15
  90.2 1.9 collective-permute-start.16
  92.2 6.3 %collective-permute-start.17 = (f32[4,1,512]{2,1,0:T(1,128)S(1)}, f32[4,1,512]{2,1,0:T(1,128)S(1)}, u32[]{:S(2)}, u32[]{:S(2)}) collective-permute-start(f32[4,1,512]{2,1,0:T(1,128)S(1)} %get-tuple-element.253), channel_id=1, source_target_pairs={{1,0},{2,1},{3,2},{4,3},{5,4},{6,5},{7,6},{8,7},{9,8},{10,9},{11,1... | collective-permute-start | bytes 24584 | tf_op jit(solution)/shard_map/ppermute | solution.py:22
  98.6 1.3 collective-permute-done.17
  100.8 2.6 stack.459
  103.4 6.6 %all-to-all-start = ((f32[16,1,4,32,512]{4,3,2,1,0:T(8,128)}), f32[16,1,4,32,512]{4,3,2,1,0:T(8,128)}, u32[]{:S(2)}, u32[]{:S(2)}) async-start(f32[16,1,4,32,512]{4,3,2,1,0:T(8,128)} %stack.459), calls=%async_computation | async-start | bytes 8388608 | tf_op jit(solution)/shard_map/all_to_all | solution.py:94
  113.3 36.9 %psum.7 = f32[]{:T(128)} all-reduce(f32[]{:T(128)} %fusion.151), channel_id=1, replica_groups=mesh['member'=16,'domain'=16] {'domain'}, use_global_device_ids=true, to_apply=%region_1.2 | all-reduce | flops 1 | bytes 8 | tf_op jit(solution)/shard_map/psum | solution.py:91
  150.9 11.6 %all-to-all-done = f32[16,1,4,32,512]{4,3,2,1,0:T(8,128)} async-done(((f32[16,1,4,32,512]{4,3,2,1,0:T(8,128)}), f32[16,1,4,32,512]{4,3,2,1,0:T(8,128)}, u32[]{:S(2)}, u32[]{:S(2)}) %all-to-all-start) | async-done | bytes 4194336 | tf_op jit(solution)/shard_map/all_to_all | solution.py:94
  162.5 1.0 bitcast_add_fusion
  163.7 1.9 collective-permute-start.18
  165.6 6.9 %collective-permute-start.19 = (f32[4,1,512]{2,1,0:T(1,128)S(1)}, f32[4,1,512]{2,1,0:T(1,128)S(1)}, u32[]{:S(2)}, u32[]{:S(2)}) collective-permute-start(f32[4,1,512]{2,1,0:T(1,128)S(1)} %get-tuple-element.244), channel_id=1, source_target_pairs={{1,0},{2,1},{3,2},{4,3},{5,4},{6,5},{7,6},{8,7},{9,8},{10,9},{11,1... | collective-permute-start | bytes 24584 | tf_op jit(solution)/shard_map/ppermute | solution.py:22
  172.6 1.3 collective-permute-done.19
  174.7 1.9 collective-permute-start.20
  176.7 6.3 %collective-permute-start.21 = (f32[4,1,512]{2,1,0:T(1,128)S(1)}, f32[4,1,512]{2,1,0:T(1,128)S(1)}, u32[]{:S(2)}, u32[]{:S(2)}) collective-permute-start(f32[4,1,512]{2,1,0:T(1,128)S(1)} %get-tuple-element.235), channel_id=1, source_target_pairs={{1,0},{2,1},{3,2},{4,3},{5,4},{6,5},{7,6},{8,7},{9,8},{10,9},{11,1... | collective-permute-start | bytes 24584 | tf_op jit(solution)/shard_map/ppermute | solution.py:22
  183.1 1.3 collective-permute-done.21
  185.2 1.9 collective-permute-start.22
  187.1 6.3 %collective-permute-start.23 = (f32[4,1,512]{2,1,0:T(1,128)S(1)}, f32[4,1,512]{2,1,0:T(1,128)S(1)}, u32[]{:S(2)}, u32[]{:S(2)}) collective-permute-start(f32[4,1,512]{2,1,0:T(1,128)S(1)} %get-tuple-element.226), channel_id=1, source_target_pairs={{1,0},{2,1},{3,2},{4,3},{5,4},{6,5},{7,6},{8,7},{9,8},{10,9},{11,1... | collective-permute-start | bytes 24584 | tf_op jit(solution)/shard_map/ppermute | solution.py:22
  193.5 1.3 collective-permute-done.23
  195.7 1.9 collective-permute-start.24
  197.7 6.3 %collective-permute-start.25 = (f32[4,1,512]{2,1,0:T(1,128)S(1)}, f32[4,1,512]{2,1,0:T(1,128)S(1)}, u32[]{:S(2)}, u32[]{:S(2)}) collective-permute-start(f32[4,1,512]{2,1,0:T(1,128)S(1)} %get-tuple-element.217), channel_id=1, source_target_pairs={{1,0},{2,1},{3,2},{4,3},{5,4},{6,5},{7,6},{8,7},{9,8},{10,9},{11,1... | collective-permute-start | bytes 24584 | tf_op jit(solution)/shard_map/ppermute | solution.py:22
  204.0 1.3 collective-permute-done.25
  206.2 1.9 collective-permute-start.26
  208.1 6.5 %collective-permute-start.27 = (f32[4,1,512]{2,1,0:T(1,128)S(1)}, f32[4,1,512]{2,1,0:T(1,128)S(1)}, u32[]{:S(2)}, u32[]{:S(2)}) collective-permute-start(f32[4,1,512]{2,1,0:T(1,128)S(1)} %get-tuple-element.208), channel_id=1, source_target_pairs={{1,0},{2,1},{3,2},{4,3},{5,4},{6,5},{7,6},{8,7},{9,8},{10,9},{11,1... | collective-permute-start | bytes 24584 | tf_op jit(solution)/shard_map/ppermute | solution.py:22
  214.7 1.1 collective-permute-done.27
  216.6 1.9 collective-permute-start.28
  218.5 6.3 %collective-permute-start.29 = (f32[4,1,512]{2,1,0:T(1,128)S(1)}, f32[4,1,512]{2,1,0:T(1,128)S(1)}, u32[]{:S(2)}, u32[]{:S(2)}) collective-permute-start(f32[4,1,512]{2,1,0:T(1,128)S(1)} %get-tuple-element.199), channel_id=1, source_target_pairs={{1,0},{2,1},{3,2},{4,3},{5,4},{6,5},{7,6},{8,7},{9,8},{10,9},{11,1... | collective-permute-start | bytes 24584 | tf_op jit(solution)/shard_map/ppermute | solution.py:22
  224.9 1.3 collective-permute-done.29
  227.1 1.9 collective-permute-start.30
  229.0 6.3 %collective-permute-start.31 = (f32[4,1,512]{2,1,0:T(1,128)S(1)}, f32[4,1,512]{2,1,0:T(1,128)S(1)}, u32[]{:S(2)}, u32[]{:S(2)}) collective-permute-start(f32[4,1,512]{2,1,0:T(1,128)S(1)} %get-tuple-element.190), channel_id=1, source_target_pairs={{1,0},{2,1},{3,2},{4,3},{5,4},{6,5},{7,6},{8,7},{9,8},{10,9},{11,1... | collective-permute-start | bytes 24584 | tf_op jit(solution)/shard_map/ppermute | solution.py:22
  235.4 1.3 collective-permute-done.31
  237.5 1.9 collective-permute-start.32
  239.4 6.3 %collective-permute-start.33 = (f32[4,1,512]{2,1,0:T(1,128)S(1)}, f32[4,1,512]{2,1,0:T(1,128)S(1)}, u32[]{:S(2)}, u32[]{:S(2)}) collective-permute-start(f32[4,1,512]{2,1,0:T(1,128)S(1)} %get-tuple-element.181), channel_id=1, source_target_pairs={{1,0},{2,1},{3,2},{4,3},{5,4},{6,5},{7,6},{8,7},{9,8},{10,9},{11,1... | collective-permute-start | bytes 24584 | tf_op jit(solution)/shard_map/ppermute | solution.py:22
  245.8 1.3 collective-permute-done.33
  248.0 1.9 collective-permute-start.34
  249.9 6.3 %collective-permute-start.35 = (f32[4,1,512]{2,1,0:T(1,128)S(1)}, f32[4,1,512]{2,1,0:T(1,128)S(1)}, u32[]{:S(2)}, u32[]{:S(2)}) collective-permute-start(f32[4,1,512]{2,1,0:T(1,128)S(1)} %get-tuple-element.172), channel_id=1, source_target_pairs={{1,0},{2,1},{3,2},{4,3},{5,4},{6,5},{7,6},{8,7},{9,8},{10,9},{11,1... | collective-permute-start | bytes 24584 | tf_op jit(solution)/shard_map/ppermute | solution.py:22
  256.3 1.3 collective-permute-done.35
  258.1 2.1 fusion.74
  (203 shorter events, 18.0 us)
Async XLA Ops:
  0.6 16.3 %copy-start = (f32[1,4,32,512]{3,2,1,0:T(8,128)S(1)}, f32[1,4,32,512]{3,2,1,0:T(8,128)}, u32[]{:S(2)}) copy-start(f32[1,4,32,512]{3,2,1,0:T(8,128)} %param.3) | copy-start | bytes 786436
  1.6 12.7 %collective-permute-start = (f32[4,1,512]{2,1,0:T(1,128)S(1)}, f32[4,1,512]{2,1,0:T(1,128)S(1)}, u32[]{:S(2)}, u32[]{:S(2)}) collective-permute-start(f32[4,1,512]{2,1,0:T(1,128)S(1)} %get-tuple-element.324), channel_id=1, source_target_pairs={{0,1},{1,2},{2,3},{3,4},{4,5},{5,6},{6,7},{7,8},{8,9},{9,10},{10,1... | collective-permute-start | bytes 24584 | tf_op jit(solution)/shard_map/ppermute | solution.py:20
  5.4 8.9 %collective-permute-start.1 = (f32[4,1,512]{2,1,0:T(1,128)S(1)}, f32[4,1,512]{2,1,0:T(1,128)S(1)}, u32[]{:S(2)}, u32[]{:S(2)}) collective-permute-start(f32[4,1,512]{2,1,0:T(1,128)S(1)} %get-tuple-element.325), channel_id=1, source_target_pairs={{1,0},{2,1},{3,2},{4,3},{5,4},{6,5},{7,6},{8,7},{9,8},{10,9},{11,1... | collective-permute-start | bytes 24584 | tf_op jit(solution)/shard_map/ppermute | solution.py:22
  17.2 8.1 %collective-permute-start.2 = (f32[4,1,512]{2,1,0:T(1,128)S(1)}, f32[4,1,512]{2,1,0:T(1,128)S(1)}, u32[]{:S(2)}, u32[]{:S(2)}) collective-permute-start(f32[4,1,512]{2,1,0:T(1,128)S(1)} %get-tuple-element.315), channel_id=1, source_target_pairs={{0,1},{1,2},{2,3},{3,4},{4,5},{5,6},{6,7},{7,8},{8,9},{9,10},{10,1... | collective-permute-start | bytes 24584 | tf_op jit(solution)/shard_map/ppermute | solution.py:20
  19.2 7.4 %collective-permute-start.3 = (f32[4,1,512]{2,1,0:T(1,128)S(1)}, f32[4,1,512]{2,1,0:T(1,128)S(1)}, u32[]{:S(2)}, u32[]{:S(2)}) collective-permute-start(f32[4,1,512]{2,1,0:T(1,128)S(1)} %get-tuple-element.316), channel_id=1, source_target_pairs={{1,0},{2,1},{3,2},{4,3},{5,4},{6,5},{7,6},{8,7},{9,8},{10,9},{11,1... | collective-permute-start | bytes 24584 | tf_op jit(solution)/shard_map/ppermute | solution.py:22
  27.4 8.3 %collective-permute-start.4 = (f32[4,1,512]{2,1,0:T(1,128)S(1)}, f32[4,1,512]{2,1,0:T(1,128)S(1)}, u32[]{:S(2)}, u32[]{:S(2)}) collective-permute-start(f32[4,1,512]{2,1,0:T(1,128)S(1)} %get-tuple-element.306), channel_id=1, source_target_pairs={{0,1},{1,2},{2,3},{3,4},{4,5},{5,6},{6,7},{7,8},{8,9},{9,10},{10,1... | collective-permute-start | bytes 24584 | tf_op jit(solution)/shard_map/ppermute | solution.py:20
  30.3 6.7 %collective-permute-start.5 = (f32[4,1,512]{2,1,0:T(1,128)S(1)}, f32[4,1,512]{2,1,0:T(1,128)S(1)}, u32[]{:S(2)}, u32[]{:S(2)}) collective-permute-start(f32[4,1,512]{2,1,0:T(1,128)S(1)} %get-tuple-element.307), channel_id=1, source_target_pairs={{1,0},{2,1},{3,2},{4,3},{5,4},{6,5},{7,6},{8,7},{9,8},{10,9},{11,1... | collective-permute-start | bytes 24584 | tf_op jit(solution)/shard_map/ppermute | solution.py:22
  38.0 8.3 %collective-permute-start.6 = (f32[4,1,512]{2,1,0:T(1,128)S(1)}, f32[4,1,512]{2,1,0:T(1,128)S(1)}, u32[]{:S(2)}, u32[]{:S(2)}) collective-permute-start(f32[4,1,512]{2,1,0:T(1,128)S(1)} %get-tuple-element.297), channel_id=1, source_target_pairs={{0,1},{1,2},{2,3},{3,4},{4,5},{5,6},{6,7},{7,8},{8,9},{9,10},{10,1... | collective-permute-start | bytes 24584 | tf_op jit(solution)/shard_map/ppermute | solution.py:20
  41.4 6.2 %collective-permute-start.7 = (f32[4,1,512]{2,1,0:T(1,128)S(1)}, f32[4,1,512]{2,1,0:T(1,128)S(1)}, u32[]{:S(2)}, u32[]{:S(2)}) collective-permute-start(f32[4,1,512]{2,1,0:T(1,128)S(1)} %get-tuple-element.298), channel_id=1, source_target_pairs={{1,0},{2,1},{3,2},{4,3},{5,4},{6,5},{7,6},{8,7},{9,8},{10,9},{11,1... | collective-permute-start | bytes 24584 | tf_op jit(solution)/shard_map/ppermute | solution.py:22
  48.4 8.3 %collective-permute-start.8 = (f32[4,1,512]{2,1,0:T(1,128)S(1)}, f32[4,1,512]{2,1,0:T(1,128)S(1)}, u32[]{:S(2)}, u32[]{:S(2)}) collective-permute-start(f32[4,1,512]{2,1,0:T(1,128)S(1)} %get-tuple-element.288), channel_id=1, source_target_pairs={{0,1},{1,2},{2,3},{3,4},{4,5},{5,6},{6,7},{7,8},{8,9},{9,10},{10,1... | collective-permute-start | bytes 24584 | tf_op jit(solution)/shard_map/ppermute | solution.py:20
  51.7 6.3 %collective-permute-start.9 = (f32[4,1,512]{2,1,0:T(1,128)S(1)}, f32[4,1,512]{2,1,0:T(1,128)S(1)}, u32[]{:S(2)}, u32[]{:S(2)}) collective-permute-start(f32[4,1,512]{2,1,0:T(1,128)S(1)} %get-tuple-element.289), channel_id=1, source_target_pairs={{1,0},{2,1},{3,2},{4,3},{5,4},{6,5},{7,6},{8,7},{9,8},{10,9},{11,1... | collective-permute-start | bytes 24584 | tf_op jit(solution)/shard_map/ppermute | solution.py:22
  58.8 8.3 %collective-permute-start.10 = (f32[4,1,512]{2,1,0:T(1,128)S(1)}, f32[4,1,512]{2,1,0:T(1,128)S(1)}, u32[]{:S(2)}, u32[]{:S(2)}) collective-permute-start(f32[4,1,512]{2,1,0:T(1,128)S(1)} %get-tuple-element.279), channel_id=1, source_target_pairs={{0,1},{1,2},{2,3},{3,4},{4,5},{5,6},{6,7},{7,8},{8,9},{9,10},{10,1... | collective-permute-start | bytes 24584 | tf_op jit(solution)/shard_map/ppermute | solution.py:20
  61.3 7.2 %collective-permute-start.11 = (f32[4,1,512]{2,1,0:T(1,128)S(1)}, f32[4,1,512]{2,1,0:T(1,128)S(1)}, u32[]{:S(2)}, u32[]{:S(2)}) collective-permute-start(f32[4,1,512]{2,1,0:T(1,128)S(1)} %get-tuple-element.280), channel_id=1, source_target_pairs={{1,0},{2,1},{3,2},{4,3},{5,4},{6,5},{7,6},{8,7},{9,8},{10,9},{11,1... | collective-permute-start | bytes 24584 | tf_op jit(solution)/shard_map/ppermute | solution.py:22
  69.4 8.3 %collective-permute-start.12 = (f32[4,1,512]{2,1,0:T(1,128)S(1)}, f32[4,1,512]{2,1,0:T(1,128)S(1)}, u32[]{:S(2)}, u32[]{:S(2)}) collective-permute-start(f32[4,1,512]{2,1,0:T(1,128)S(1)} %get-tuple-element.270), channel_id=1, source_target_pairs={{0,1},{1,2},{2,3},{3,4},{4,5},{5,6},{6,7},{7,8},{8,9},{9,10},{10,1... | collective-permute-start | bytes 24584 | tf_op jit(solution)/shard_map/ppermute | solution.py:20
  71.3 7.7 %collective-permute-start.13 = (f32[4,1,512]{2,1,0:T(1,128)S(1)}, f32[4,1,512]{2,1,0:T(1,128)S(1)}, u32[]{:S(2)}, u32[]{:S(2)}) collective-permute-start(f32[4,1,512]{2,1,0:T(1,128)S(1)} %get-tuple-element.271), channel_id=1, source_target_pairs={{1,0},{2,1},{3,2},{4,3},{5,4},{6,5},{7,6},{8,7},{9,8},{10,9},{11,1... | collective-permute-start | bytes 24584 | tf_op jit(solution)/shard_map/ppermute | solution.py:22
  79.8 8.3 %collective-permute-start.14 = (f32[4,1,512]{2,1,0:T(1,128)S(1)}, f32[4,1,512]{2,1,0:T(1,128)S(1)}, u32[]{:S(2)}, u32[]{:S(2)}) collective-permute-start(f32[4,1,512]{2,1,0:T(1,128)S(1)} %get-tuple-element.261), channel_id=1, source_target_pairs={{0,1},{1,2},{2,3},{3,4},{4,5},{5,6},{6,7},{7,8},{8,9},{9,10},{10,1... | collective-permute-start | bytes 24584 | tf_op jit(solution)/shard_map/ppermute | solution.py:20
  81.7 7.7 %collective-permute-start.15 = (f32[4,1,512]{2,1,0:T(1,128)S(1)}, f32[4,1,512]{2,1,0:T(1,128)S(1)}, u32[]{:S(2)}, u32[]{:S(2)}) collective-permute-start(f32[4,1,512]{2,1,0:T(1,128)S(1)} %get-tuple-element.262), channel_id=1, source_target_pairs={{1,0},{2,1},{3,2},{4,3},{5,4},{6,5},{7,6},{8,7},{9,8},{10,9},{11,1... | collective-permute-start | bytes 24584 | tf_op jit(solution)/shard_map/ppermute | solution.py:22
  90.2 8.3 %collective-permute-start.16 = (f32[4,1,512]{2,1,0:T(1,128)S(1)}, f32[4,1,512]{2,1,0:T(1,128)S(1)}, u32[]{:S(2)}, u32[]{:S(2)}) collective-permute-start(f32[4,1,512]{2,1,0:T(1,128)S(1)} %get-tuple-element.252), channel_id=1, source_target_pairs={{0,1},{1,2},{2,3},{3,4},{4,5},{5,6},{6,7},{7,8},{8,9},{9,10},{10,1... | collective-permute-start | bytes 24584 | tf_op jit(solution)/shard_map/ppermute | solution.py:20
  92.2 7.7 %collective-permute-start.17 = (f32[4,1,512]{2,1,0:T(1,128)S(1)}, f32[4,1,512]{2,1,0:T(1,128)S(1)}, u32[]{:S(2)}, u32[]{:S(2)}) collective-permute-start(f32[4,1,512]{2,1,0:T(1,128)S(1)} %get-tuple-element.253), channel_id=1, source_target_pairs={{1,0},{2,1},{3,2},{4,3},{5,4},{6,5},{7,6},{8,7},{9,8},{10,9},{11,1... | collective-permute-start | bytes 24584 | tf_op jit(solution)/shard_map/ppermute | solution.py:22
  103.4 6.6 %copy-start.2 = (s32[16]{0:T(128)S(1)}, s32[16]{0:T(128)}, u32[]{:S(2)}) copy-start(s32[16]{0:T(128)} %param.5) | copy-start | bytes 196
  103.4 59.0 %copy-start.1 = (f32[1,4,32,512]{3,2,1,0:T(8,128)S(1)}, f32[1,4,32,512]{3,2,1,0:T(8,128)}, u32[]{:S(2)}) copy-start(f32[1,4,32,512]{3,2,1,0:T(8,128)} %param.4) | copy-start | bytes 786436
  103.4 59.0 %all-to-all-start = ((f32[16,1,4,32,512]{4,3,2,1,0:T(8,128)}), f32[16,1,4,32,512]{4,3,2,1,0:T(8,128)}, u32[]{:S(2)}, u32[]{:S(2)}) async-start(f32[16,1,4,32,512]{4,3,2,1,0:T(8,128)} %stack.459), calls=%async_computation | async-start | bytes 8388608 | tf_op jit(solution)/shard_map/all_to_all | solution.py:94
  163.7 8.9 %collective-permute-start.18 = (f32[4,1,512]{2,1,0:T(1,128)S(1)}, f32[4,1,512]{2,1,0:T(1,128)S(1)}, u32[]{:S(2)}, u32[]{:S(2)}) collective-permute-start(f32[4,1,512]{2,1,0:T(1,128)S(1)} %get-tuple-element.243), channel_id=1, source_target_pairs={{0,1},{1,2},{2,3},{3,4},{4,5},{5,6},{6,7},{7,8},{8,9},{9,10},{10,1... | collective-permute-start | bytes 24584 | tf_op jit(solution)/shard_map/ppermute | solution.py:20
  165.6 8.3 %collective-permute-start.19 = (f32[4,1,512]{2,1,0:T(1,128)S(1)}, f32[4,1,512]{2,1,0:T(1,128)S(1)}, u32[]{:S(2)}, u32[]{:S(2)}) collective-permute-start(f32[4,1,512]{2,1,0:T(1,128)S(1)} %get-tuple-element.244), channel_id=1, source_target_pairs={{1,0},{2,1},{3,2},{4,3},{5,4},{6,5},{7,6},{8,7},{9,8},{10,9},{11,1... | collective-permute-start | bytes 24584 | tf_op jit(solution)/shard_map/ppermute | solution.py:22
  174.7 8.3 %collective-permute-start.20 = (f32[4,1,512]{2,1,0:T(1,128)S(1)}, f32[4,1,512]{2,1,0:T(1,128)S(1)}, u32[]{:S(2)}, u32[]{:S(2)}) collective-permute-start(f32[4,1,512]{2,1,0:T(1,128)S(1)} %get-tuple-element.234), channel_id=1, source_target_pairs={{0,1},{1,2},{2,3},{3,4},{4,5},{5,6},{6,7},{7,8},{8,9},{9,10},{10,1... | collective-permute-start | bytes 24584 | tf_op jit(solution)/shard_map/ppermute | solution.py:20
  176.7 7.7 %collective-permute-start.21 = (f32[4,1,512]{2,1,0:T(1,128)S(1)}, f32[4,1,512]{2,1,0:T(1,128)S(1)}, u32[]{:S(2)}, u32[]{:S(2)}) collective-permute-start(f32[4,1,512]{2,1,0:T(1,128)S(1)} %get-tuple-element.235), channel_id=1, source_target_pairs={{1,0},{2,1},{3,2},{4,3},{5,4},{6,5},{7,6},{8,7},{9,8},{10,9},{11,1... | collective-permute-start | bytes 24584 | tf_op jit(solution)/shard_map/ppermute | solution.py:22
  185.2 8.3 %collective-permute-start.22 = (f32[4,1,512]{2,1,0:T(1,128)S(1)}, f32[4,1,512]{2,1,0:T(1,128)S(1)}, u32[]{:S(2)}, u32[]{:S(2)}) collective-permute-start(f32[4,1,512]{2,1,0:T(1,128)S(1)} %get-tuple-element.225), channel_id=1, source_target_pairs={{0,1},{1,2},{2,3},{3,4},{4,5},{5,6},{6,7},{7,8},{8,9},{9,10},{10,1... | collective-permute-start | bytes 24584 | tf_op jit(solution)/shard_map/ppermute | solution.py:20
  187.1 7.7 %collective-permute-start.23 = (f32[4,1,512]{2,1,0:T(1,128)S(1)}, f32[4,1,512]{2,1,0:T(1,128)S(1)}, u32[]{:S(2)}, u32[]{:S(2)}) collective-permute-start(f32[4,1,512]{2,1,0:T(1,128)S(1)} %get-tuple-element.226), channel_id=1, source_target_pairs={{1,0},{2,1},{3,2},{4,3},{5,4},{6,5},{7,6},{8,7},{9,8},{10,9},{11,1... | collective-permute-start | bytes 24584 | tf_op jit(solution)/shard_map/ppermute | solution.py:22
  195.7 8.3 %collective-permute-start.24 = (f32[4,1,512]{2,1,0:T(1,128)S(1)}, f32[4,1,512]{2,1,0:T(1,128)S(1)}, u32[]{:S(2)}, u32[]{:S(2)}) collective-permute-start(f32[4,1,512]{2,1,0:T(1,128)S(1)} %get-tuple-element.216), channel_id=1, source_target_pairs={{0,1},{1,2},{2,3},{3,4},{4,5},{5,6},{6,7},{7,8},{8,9},{9,10},{10,1... | collective-permute-start | bytes 24584 | tf_op jit(solution)/shard_map/ppermute | solution.py:20
  197.7 7.7 %collective-permute-start.25 = (f32[4,1,512]{2,1,0:T(1,128)S(1)}, f32[4,1,512]{2,1,0:T(1,128)S(1)}, u32[]{:S(2)}, u32[]{:S(2)}) collective-permute-start(f32[4,1,512]{2,1,0:T(1,128)S(1)} %get-tuple-element.217), channel_id=1, source_target_pairs={{1,0},{2,1},{3,2},{4,3},{5,4},{6,5},{7,6},{8,7},{9,8},{10,9},{11,1... | collective-permute-start | bytes 24584 | tf_op jit(solution)/shard_map/ppermute | solution.py:22
  206.2 8.5 %collective-permute-start.26 = (f32[4,1,512]{2,1,0:T(1,128)S(1)}, f32[4,1,512]{2,1,0:T(1,128)S(1)}, u32[]{:S(2)}, u32[]{:S(2)}) collective-permute-start(f32[4,1,512]{2,1,0:T(1,128)S(1)} %get-tuple-element.207), channel_id=1, source_target_pairs={{0,1},{1,2},{2,3},{3,4},{4,5},{5,6},{6,7},{7,8},{8,9},{9,10},{10,1... | collective-permute-start | bytes 24584 | tf_op jit(solution)/shard_map/ppermute | solution.py:20
  208.1 7.7 %collective-permute-start.27 = (f32[4,1,512]{2,1,0:T(1,128)S(1)}, f32[4,1,512]{2,1,0:T(1,128)S(1)}, u32[]{:S(2)}, u32[]{:S(2)}) collective-permute-start(f32[4,1,512]{2,1,0:T(1,128)S(1)} %get-tuple-element.208), channel_id=1, source_target_pairs={{1,0},{2,1},{3,2},{4,3},{5,4},{6,5},{7,6},{8,7},{9,8},{10,9},{11,1... | collective-permute-start | bytes 24584 | tf_op jit(solution)/shard_map/ppermute | solution.py:22
  216.6 8.3 %collective-permute-start.28 = (f32[4,1,512]{2,1,0:T(1,128)S(1)}, f32[4,1,512]{2,1,0:T(1,128)S(1)}, u32[]{:S(2)}, u32[]{:S(2)}) collective-permute-start(f32[4,1,512]{2,1,0:T(1,128)S(1)} %get-tuple-element.198), channel_id=1, source_target_pairs={{0,1},{1,2},{2,3},{3,4},{4,5},{5,6},{6,7},{7,8},{8,9},{9,10},{10,1... | collective-permute-start | bytes 24584 | tf_op jit(solution)/shard_map/ppermute | solution.py:20
  218.5 7.7 %collective-permute-start.29 = (f32[4,1,512]{2,1,0:T(1,128)S(1)}, f32[4,1,512]{2,1,0:T(1,128)S(1)}, u32[]{:S(2)}, u32[]{:S(2)}) collective-permute-start(f32[4,1,512]{2,1,0:T(1,128)S(1)} %get-tuple-element.199), channel_id=1, source_target_pairs={{1,0},{2,1},{3,2},{4,3},{5,4},{6,5},{7,6},{8,7},{9,8},{10,9},{11,1... | collective-permute-start | bytes 24584 | tf_op jit(solution)/shard_map/ppermute | solution.py:22
  227.1 8.3 %collective-permute-start.30 = (f32[4,1,512]{2,1,0:T(1,128)S(1)}, f32[4,1,512]{2,1,0:T(1,128)S(1)}, u32[]{:S(2)}, u32[]{:S(2)}) collective-permute-start(f32[4,1,512]{2,1,0:T(1,128)S(1)} %get-tuple-element.189), channel_id=1, source_target_pairs={{0,1},{1,2},{2,3},{3,4},{4,5},{5,6},{6,7},{7,8},{8,9},{9,10},{10,1... | collective-permute-start | bytes 24584 | tf_op jit(solution)/shard_map/ppermute | solution.py:20
  229.0 7.7 %collective-permute-start.31 = (f32[4,1,512]{2,1,0:T(1,128)S(1)}, f32[4,1,512]{2,1,0:T(1,128)S(1)}, u32[]{:S(2)}, u32[]{:S(2)}) collective-permute-start(f32[4,1,512]{2,1,0:T(1,128)S(1)} %get-tuple-element.190), channel_id=1, source_target_pairs={{1,0},{2,1},{3,2},{4,3},{5,4},{6,5},{7,6},{8,7},{9,8},{10,9},{11,1... | collective-permute-start | bytes 24584 | tf_op jit(solution)/shard_map/ppermute | solution.py:22
  237.5 8.3 %collective-permute-start.32 = (f32[4,1,512]{2,1,0:T(1,128)S(1)}, f32[4,1,512]{2,1,0:T(1,128)S(1)}, u32[]{:S(2)}, u32[]{:S(2)}) collective-permute-start(f32[4,1,512]{2,1,0:T(1,128)S(1)} %get-tuple-element.180), channel_id=1, source_target_pairs={{0,1},{1,2},{2,3},{3,4},{4,5},{5,6},{6,7},{7,8},{8,9},{9,10},{10,1... | collective-permute-start | bytes 24584 | tf_op jit(solution)/shard_map/ppermute | solution.py:20
  239.4 7.7 %collective-permute-start.33 = (f32[4,1,512]{2,1,0:T(1,128)S(1)}, f32[4,1,512]{2,1,0:T(1,128)S(1)}, u32[]{:S(2)}, u32[]{:S(2)}) collective-permute-start(f32[4,1,512]{2,1,0:T(1,128)S(1)} %get-tuple-element.181), channel_id=1, source_target_pairs={{1,0},{2,1},{3,2},{4,3},{5,4},{6,5},{7,6},{8,7},{9,8},{10,9},{11,1... | collective-permute-start | bytes 24584 | tf_op jit(solution)/shard_map/ppermute | solution.py:22
  248.0 8.3 %collective-permute-start.34 = (f32[4,1,512]{2,1,0:T(1,128)S(1)}, f32[4,1,512]{2,1,0:T(1,128)S(1)}, u32[]{:S(2)}, u32[]{:S(2)}) collective-permute-start(f32[4,1,512]{2,1,0:T(1,128)S(1)} %get-tuple-element.171), channel_id=1, source_target_pairs={{0,1},{1,2},{2,3},{3,4},{4,5},{5,6},{6,7},{7,8},{8,9},{9,10},{10,1... | collective-permute-start | bytes 24584 | tf_op jit(solution)/shard_map/ppermute | solution.py:20
  249.9 7.7 %collective-permute-start.35 = (f32[4,1,512]{2,1,0:T(1,128)S(1)}, f32[4,1,512]{2,1,0:T(1,128)S(1)}, u32[]{:S(2)}, u32[]{:S(2)}) collective-permute-start(f32[4,1,512]{2,1,0:T(1,128)S(1)} %get-tuple-element.172), channel_id=1, source_target_pairs={{1,0},{2,1},{3,2},{4,3},{5,4},{6,5},{7,6},{8,7},{9,8},{10,9},{11,1... | collective-permute-start | bytes 24584 | tf_op jit(solution)/shard_map/ppermute | solution.py:22
